TPU v7x, 32 devices: a whole 2x2x4 slice. The times are simulated.
32 devices in a mesh: site: 8 (over z, x), real: 4 (over y, core).
Axes of the slice: x: 2, y: 2, z: 4, core: 2. Of those that a mesh axis runs over, the one named last changes fastest.
Arguments:
- epsilon: bfloat16 [8192, 2048], P('site', 'real'), may hold values from -6 to 6
- factor: bfloat16 [2, 72, 512, 512], P(None, 'site'), may hold values from -0.09375 to 0.09375
- block_rows: int32 [2, 72], P(None, 'site'), may hold values from 0 to 15, as said below
- median_log: float32 [8192], P('site'), may hold values from -2.5 to -0.5
- spread_log: float32 [8192], P('site'), may hold values from 0.4 to 0.8
- critical_yield: float32 [8192], P('site'), may hold values from 0.03 to 0.3
Outputs:
- residual_field: bfloat16 [8192, 2048], P('site', 'real')
- mean_damage: float32 [8192], P('site')
Inputs may be any that keep to these rules, and one draw needn't show every extreme that they name: block_rows[p, b] = (c + o) mod 16, with c = 2 * (b // 9) + p the block's column tile and o in 0 to 11; the offsets o of one block column are distinct, and the first block of each column has o = 0.
All inputs are finite; a program needn't handle non-finite values.
Results may differ from a plain program's by a relative error of at most 0.001.
Values sent between devices are 32-bit elements; how exact they have to be, the bound alone decides.
A program may use at most 256 MiB of HBM per device.

v0:
```python
import jax
import jax.numpy as jnp
from jax import lax
from jax.sharding import PartitionSpec as P

BAND = 12


coeff_disp = 10.0**0.215
power_margin = 2.341
power_ratio = 1.438


def passed_along(value, axis, steps):
    count = lax.axis_size(axis)
    pairs = [(source, (source + steps) % count) for source in range(count)]
    return lax.ppermute(value, axis, pairs)


def shards(epsilon, factor, block_rows, median_log, spread_log, critical_yield):
    panels = factor.shape[0]
    per_column = factor.shape[1]
    tile_size = factor.shape[-1]
    own_reals = epsilon.shape[1]
    reach = BAND // 2
    own_index = lax.axis_index("site")
    total_tiles = panels * lax.axis_size("site")
    draws = epsilon.reshape(panels, tile_size, own_reals)

    def pending(panel):
        flat = factor[panel].reshape(per_column * tile_size, tile_size)
        products = jnp.dot(flat, draws[panel], preferred_element_type=jnp.float32)
        products = products.reshape(per_column, tile_size, own_reals)
        relative = (block_rows[panel] - own_index * panels) % total_tiles
        slots = jnp.zeros(((reach + 1) * panels, tile_size, own_reals), jnp.float32)
        sums = slots.at[relative].set(products, unique_indices=True)
        return sums.reshape(reach + 1, panels, tile_size, own_reals)

    combined = pending(0)
    panel = 1
    combined = combined + pending(panel)
    arrived = combined[0]
    for offset in range(1, reach + 1):
        arrived = arrived + passed_along(combined[offset], "site", offset)
    residual_field = arrived.astype(jnp.bfloat16).reshape(panels * tile_size, own_reals)
    log_peak = median_log[:, None] + spread_log[:, None] * residual_field.astype(jnp.float32)
    log_ratio = jnp.log(critical_yield)[:, None] - log_peak
    ratio = jnp.exp(log_ratio)
    margin = jnp.maximum(1.0 - ratio, 0.0)
    displacement = coeff_disp * jnp.power(margin, power_margin) * jnp.exp(-power_ratio * log_ratio)
    local_total = jnp.sum(jnp.log1p(displacement), axis=1)
    total = lax.psum(local_total, "real")
    mean_damage = total / (own_reals * lax.axis_size("real"))
    return (residual_field, mean_damage)


def solution(mesh):
    return jax.shard_map(
        shards,
        mesh=mesh,
        in_specs=(
            P("site", "real"),
            P(None, "site", None, None),
            P(None, "site"),
            P("site"),
            P("site"),
            P("site"),
        ),
        out_specs=(P("site", "real"), P("site")),
        check_vma=False,
    )
```

profile of v0, /device:TPU:10, one launch (start us, length us, event | category | flops | bytes accessed | tf_op | source)
XLA Modules:
  0.0 466.7 jit_solution(16019307224608560952)
XLA Ops:
  0.6 0.0 copy-start
  0.7 8.9 %fusion.2 = f32[9,512,512]{2,1,0:T(8,128)} fusion(bf16[2,9,512,512]{3,2,1,0:T(8,128)(2,1)} %param.7, bf16[1024,512]{1,0:T(8,128)(2,1)} %param.6), kind=kOutput, calls=%fused_computation.4 | convolution fusion | flops 2415919104 | bytes 14680064 | tf_op jit(solution)/shard_map/dot_general | solution.py:32
  9.6 5.0 %fusion = f32[9,512,512]{2,1,0:T(8,128)} fusion(bf16[2,9,512,512]{3,2,1,0:T(8,128)(2,1)S(1)} %copy-done, bf16[1024,512]{1,0:T(8,128)(2,1)S(1)} %copy-done.1), kind=kOutput, calls=%fused_computation.2 | convolution fusion | flops 2415919104 | bytes 14680064 | tf_op jit(solution)/shard_map/dot_general | solution.py:32
  14.6 7.0 %broadcast.141.clone = f32[14,512,512]{2,1,0:T(8,128)} broadcast(f32[]{:T(128)} %constant.16.clone.1), dimensions={} | broadcast | bytes 14680068 | tf_op jit(solution)/shard_map/broadcast.7
  21.7 18.4 %scatter_fusion = f32[14,512,512]{2,1,0:T(8,128)} fusion(f32[14,512,512]{2,1,0:T(8,128)} %broadcast.141.clone, s32[9]{0:T(128)S(1)} %get-tuple-element.11, f32[9,512,512]{2,1,0:T(8,128)} %fusion.2), kind=kCustom, calls=%fused_computation | custom fusion | bytes 28311588 | tf_op jit(solution)/shard_map/scatter | solution.py:36
  40.1 7.1 %broadcast.141.clone.1 = f32[14,512,512]{2,1,0:T(8,128)} broadcast(f32[]{:T(128)} %constant.16.clone.1), dimensions={} | broadcast | bytes 14680068 | tf_op jit(solution)/shard_map/broadcast.7
  47.1 18.3 %scatter_fusion.1 = f32[14,512,512]{2,1,0:T(8,128)} fusion(f32[14,512,512]{2,1,0:T(8,128)} %broadcast.141.clone.1, s32[9]{0:T(128)S(1)} %get-tuple-element.10, f32[9,512,512]{2,1,0:T(8,128)} %fusion), kind=kCustom, calls=%fused_computation.1 | custom fusion | bytes 28311588 | tf_op jit(solution)/shard_map/scatter | solution.py:36
  65.4 15.0 %add.83 = f32[14,512,512]{2,1,0:T(8,128)} add(f32[14,512,512]{2,1,0:T(8,128)} %scatter_fusion, f32[14,512,512]{2,1,0:T(8,128)} %scatter_fusion.1) | non-fusion elementwise | flops 3670016 | bytes 44040192 | tf_op jit(solution)/shard_map/add | solution.py:41
  80.4 8.7 %fusion.21 = (f32[2,512,512]{2,1,0:T(8,128)S(1)}, f32[2,512,512]{2,1,0:T(8,128)}, f32[2,512,512]{2,1,0:T(8,128)}, f32[2,512,512]{2,1,0:T(8,128)}, f32[2,512,512]{2,1,0:T(8,128)}, /*index=5*/f32[2,512,512]{2,1,0:T(8,128)}) fusion(f32[14,512,512]{2,1,0:T(8,128)} %add.83), kind=kLoop, calls=%fused_computation.33 | loop fusion | bytes 25165824 | tf_op jit(solution)/shard_map/slice | solution.py:44
  89.1 1.4 collective-permute-start
  90.6 1.7 collective-permute-start.1
  92.3 1.1 collective-permute-start.2
  93.4 1.7 collective-permute-start.3
  95.1 1.2 collective-permute-start.4
  96.3 40.3 %collective-permute-done = f32[2,512,512]{2,1,0:T(8,128)S(1)} collective-permute-done((f32[2,512,512]{2,1,0:T(8,128)S(1)}, f32[2,512,512]{2,1,0:T(8,128)S(1)}, u32[]{:S(2)}, u32[]{:S(2)}) %collective-permute-start) | collective-permute-done | bytes 2097184 | tf_op jit(solution)/shard_map/ppermute | solution.py:17
  136.6 0.4 collective-permute-start.5
  137.1 224.3 %collective-permute-done.1 = f32[2,512,512]{2,1,0:T(8,128)} collective-permute-done((f32[2,512,512]{2,1,0:T(8,128)}, f32[2,512,512]{2,1,0:T(8,128)}, u32[]{:S(2)}, u32[]{:S(2)}) %collective-permute-start.1) | collective-permute-done | bytes 2097184 | tf_op jit(solution)/shard_map/ppermute | solution.py:17
  361.4 44.9 %collective-permute-done.2 = f32[2,512,512]{2,1,0:T(8,128)} collective-permute-done((f32[2,512,512]{2,1,0:T(8,128)}, f32[2,512,512]{2,1,0:T(8,128)}, u32[]{:S(2)}, u32[]{:S(2)}) %collective-permute-start.2) | collective-permute-done | bytes 2097184 | tf_op jit(solution)/shard_map/ppermute | solution.py:17
  406.3 43.8 %collective-permute-done.3 = f32[2,512,512]{2,1,0:T(8,128)} collective-permute-done((f32[2,512,512]{2,1,0:T(8,128)}, f32[2,512,512]{2,1,0:T(8,128)}, u32[]{:S(2)}, u32[]{:S(2)}) %collective-permute-start.3) | collective-permute-done | bytes 2097184 | tf_op jit(solution)/shard_map/ppermute | solution.py:17
  450.1 0.0 collective-permute-done.4
  450.1 2.0 collective-permute-done.5
  452.1 7.0 %log-plus-one_reduce_fusion = (f32[2,512]{1,0:T(2,128)S(1)}, bf16[2,512,512]{2,1,0:T(8,128)(2,1)}) fusion(f32[2,512]{1,0:T(2,128)S(1)} %mul.34, f32[2,512]{1,0:T(2,128)S(1)} %add.90, f32[2,512]{1,0:T(2,128)S(1)} %sub.54, f32[2,512,512]{2,1,0:T(8,128)} %collective-permute-done.5, f32[2,512,512]{2,1,0:T(8,128)} %collective-permute-done.4, ...), kind=kLoop, calls=%fused_computation.15 | loop fusion | flops 8911872 | bytes 15745024 | tf_op jit(solution)/shard_map/reduce_sum | solution.py:51
  459.2 6.9 %psum.7 = f32[1024]{0:T(1024)S(1)} all-reduce(f32[1024]{0:T(1024)S(1)} %bitcast.25), channel_id=1, replica_groups=mesh['site'=8,'real'=4] {'real'}, use_global_device_ids=true, to_apply=%region_3.4 | all-reduce | flops 1024 | bytes 8192 | tf_op jit(solution)/shard_map/psum | solution.py:52
  466.1 0.6 broadcast_multiply_fusion
  (17 shorter events, 0.1 us)
Async XLA Ops:
  0.6 8.9 %copy-start = (bf16[2,9,512,512]{3,2,1,0:T(8,128)(2,1)S(1)}, bf16[2,9,512,512]{3,2,1,0:T(8,128)(2,1)}, u32[]{:S(2)}) copy-start(bf16[2,9,512,512]{3,2,1,0:T(8,128)(2,1)} %param.7) | copy-start | bytes 28311556
  0.6 8.9 %copy-start.1 = (bf16[1024,512]{1,0:T(8,128)(2,1)S(1)}, bf16[1024,512]{1,0:T(8,128)(2,1)}, u32[]{:S(2)}) copy-start(bf16[1024,512]{1,0:T(8,128)(2,1)} %param.6) | copy-start | bytes 3145732
  9.6 5.1 %copy-start.5 = (s32[2,9]{1,0:T(2,128)S(1)}, s32[2,9]{1,0:T(2,128)}, u32[]{:S(2)}) copy-start(s32[2,9]{1,0:T(2,128)} %param.8) | copy-start | bytes 220
  80.4 56.6 %copy-start.2 = (f32[1024]{0:T(1024)S(1)}, f32[1024]{0:T(1024)}, u32[]{:S(2)}) copy-start(f32[1024]{0:T(1024)} %param.11) | copy-start | bytes 12292
  80.4 56.6 %copy-start.3 = (f32[1024]{0:T(1024)S(1)}, f32[1024]{0:T(1024)}, u32[]{:S(2)}) copy-start(f32[1024]{0:T(1024)} %param.9) | copy-start | bytes 12292
  80.4 56.6 %copy-start.4 = (f32[1024]{0:T(1024)S(1)}, f32[1024]{0:T(1024)}, u32[]{:S(2)}) copy-start(f32[1024]{0:T(1024)} %param.10) | copy-start | bytes 12292
  89.1 47.5 %collective-permute-start = (f32[2,512,512]{2,1,0:T(8,128)S(1)}, f32[2,512,512]{2,1,0:T(8,128)S(1)}, u32[]{:S(2)}, u32[]{:S(2)}) collective-permute-start(f32[2,512,512]{2,1,0:T(8,128)S(1)} %get-tuple-element.4), channel_id=1, source_target_pairs={{0,4},{4,8},{8,12},{12,16},{16,20},{20,24},{24,28},{28,0},{1,5},{5... | collective-permute-start | bytes 6291464 | tf_op jit(solution)/shard_map/ppermute | solution.py:17
  90.6 270.8 %collective-permute-start.1 = (f32[2,512,512]{2,1,0:T(8,128)}, f32[2,512,512]{2,1,0:T(8,128)}, u32[]{:S(2)}, u32[]{:S(2)}) collective-permute-start(f32[2,512,512]{2,1,0:T(8,128)} %get-tuple-element.9), channel_id=1, source_target_pairs={{0,8},{4,12},{8,16},{12,20},{16,24},{20,28},{24,0},{28,4},{1,9},{5... | collective-permute-start | bytes 6291464 | tf_op jit(solution)/shard_map/ppermute | solution.py:17
  92.3 314.1 %collective-permute-start.2 = (f32[2,512,512]{2,1,0:T(8,128)}, f32[2,512,512]{2,1,0:T(8,128)}, u32[]{:S(2)}, u32[]{:S(2)}) collective-permute-start(f32[2,512,512]{2,1,0:T(8,128)} %get-tuple-element.8), channel_id=1, source_target_pairs={{0,12},{4,16},{8,20},{12,24},{16,28},{20,0},{24,4},{28,8},{1,13},{... | collective-permute-start | bytes 6291464 | tf_op jit(solution)/shard_map/ppermute | solution.py:17
  93.4 356.8 %collective-permute-start.3 = (f32[2,512,512]{2,1,0:T(8,128)}, f32[2,512,512]{2,1,0:T(8,128)}, u32[]{:S(2)}, u32[]{:S(2)}) collective-permute-start(f32[2,512,512]{2,1,0:T(8,128)} %get-tuple-element.7), channel_id=1, source_target_pairs={{0,16},{4,20},{8,24},{12,28},{16,0},{20,4},{24,8},{28,12},{1,17},{... | collective-permute-start | bytes 6291464 | tf_op jit(solution)/shard_map/ppermute | solution.py:17
  95.1 355.0 %collective-permute-start.4 = (f32[2,512,512]{2,1,0:T(8,128)}, f32[2,512,512]{2,1,0:T(8,128)}, u32[]{:S(2)}, u32[]{:S(2)}) collective-permute-start(f32[2,512,512]{2,1,0:T(8,128)} %get-tuple-element.6), channel_id=1, source_target_pairs={{0,20},{4,24},{8,28},{12,0},{16,4},{20,8},{24,12},{28,16},{1,21},{... | collective-permute-start | bytes 6291464 | tf_op jit(solution)/shard_map/ppermute | solution.py:17
  136.6 315.5 %collective-permute-start.5 = (f32[2,512,512]{2,1,0:T(8,128)}, f32[2,512,512]{2,1,0:T(8,128)}, u32[]{:S(2)}, u32[]{:S(2)}) collective-permute-start(f32[2,512,512]{2,1,0:T(8,128)} %get-tuple-element.5), channel_id=1, source_target_pairs={{0,24},{4,28},{8,0},{12,4},{16,8},{20,12},{24,16},{28,20},{1,25},{... | collective-permute-start | bytes 6291464 | tf_op jit(solution)/shard_map/ppermute | solution.py:17
where the time goes:
time: 467 us
  waiting for transfers between devices  355 us (76%)
  local copies, waits for them, and re-layouts  59.6 us (13%)
  other arithmetic  22.6 us (5%)
  matrix products  13.9 us (3%)
  starting transfers between devices  7.59 us (2%)
  blocking collectives  6.91 us (1%)
    ppermute x6, waiting for transfers between devices, passed_along(): return lax.ppermute(value, axis, pairs)  355 us
    scatter x2, local copies, waits for them, and re-layouts, pending(): sums = slots.at[relative].set(products, unique_indices=True)  36.7 us
    add x1, other arithmetic, shards(): combined = combined + pending(panel)  15 us
    another operation x2, local copies, waits for them, and re-layouts  14.1 us
    dot_general x2, matrix products, pending(): products = jnp.dot(flat, draws[panel], preferred_element_type=jnp.float32)  13.9 us
  transfers between devices with their start and end apart: 6, of which 5 were waited for; matrix products, arithmetic and copies ran while one was open for 0% of the time, Pallas kernels for 0%

commit v1 on v0

--- a/solution.py
+++ b/solution.py
@@ -1,10 +1,17 @@
+import functools
 import jax
 import jax.numpy as jnp
 from jax import lax
+from jax.experimental import pallas as pl
+from jax.experimental.pallas import tpu as pltpu
 from jax.sharding import PartitionSpec as P
 
 BAND = 12
-
+PAIR = 2
+ROWS = 128
+AHEAD = 24
+LAG = 1
+MESH = pl.DeviceIdType.MESH
 
 coeff_disp = 10.0**0.215
 power_margin = 2.341
@@ -54,9 +61,258 @@
     return (residual_field, mean_damage)
 
 
+def field_kernel(
+    depth, own_reals, table, eps_in, factor_in, median, spread, critical, field_out, mean_out,
+    eps, factor, x_out, x_in, z_out, z_in, totals,
+    load_sem, x_send, x_recv, z_send, z_recv, t_send, t_recv,
+):
+    panels, per_column, tile = factor.shape[0], factor.shape[1], factor.shape[2]
+    chunks = panels * tile // ROWS
+    per_tile = tile // ROWS
+    stages = depth - 1
+    steps = stages * chunks
+    reals = lax.axis_size("real")
+    site = lax.axis_index("site")
+    me = lax.axis_index("real")
+    z, x = site // PAIR, site % PAIR
+
+    loads = [pltpu.make_async_copy(eps_in, eps, load_sem.at[0])]
+    for panel in range(panels):
+        loads.append(pltpu.make_async_copy(factor_in.at[panel], factor.at[panel], load_sem.at[1 + panel]))
+    for load in loads:
+        load.start()
+
+    barrier = pltpu.get_barrier_semaphore()
+    pl.semaphore_signal(barrier, inc=1, device_id={"site": site + 1 - 2 * x}, device_id_type=MESH)
+    for shift in range(1, reals):
+        pl.semaphore_signal(barrier, inc=1, device_id={"real": (me + shift) % reals}, device_id_type=MESH)
+
+    @pl.when(z > 0)
+    def _():
+        pl.semaphore_signal(barrier, inc=1, device_id={"site": site - PAIR}, device_id_type=MESH)
+
+    @pl.when(z < depth - 1)
+    def _():
+        pl.semaphore_signal(barrier, inc=1, device_id={"site": site + PAIR}, device_id_type=MESH)
+
+    pl.semaphore_wait(barrier, reals + jnp.where(z > 0, 1, 0) + jnp.where(z < depth - 1, 1, 0))
+
+    for load in loads:
+        load.wait()
+
+    def partial(offset, chunk):
+        relative = panels * offset + chunk // per_tile
+        row = pl.multiple_of((chunk % per_tile) * ROWS, ROWS)
+        result = None
+        for panel in range(panels):
+            block = factor[panel, table[panel, relative], pl.ds(row, ROWS), :]
+            product = jnp.dot(
+                block, eps[panel * tile:(panel + 1) * tile, :], preferred_element_type=jnp.float32
+            ) * table[panels + panel, relative].astype(jnp.float32)
+            result = product if result is None else result + product
+        return result
+
+    low = 2 * z < depth
+
+    def target(stage):
+        falling = depth - 1 - stage
+        of_low = jnp.where(falling > z, falling, stage - (depth - 1 - z))
+        of_high = jnp.where(stage < z, stage, depth - 1 - (stage - z))
+        of_stage = jnp.where(low, of_low, of_high)
+        return jnp.where(stage == stages, z, of_stage)
+
+    skipped = jnp.where(z == 0, 0, jnp.where(low, stages - 1, z - 1))
+
+    def x_copy(group, chunk):
+        return pltpu.make_async_remote_copy(
+            src_ref=x_out.at[group, chunk],
+            dst_ref=x_in.at[group, chunk],
+            send_sem=x_send.at[group, chunk],
+            recv_sem=x_recv.at[group, chunk],
+            device_id={"site": site + 1 - 2 * x},
+            device_id_type=MESH,
+        )
+
+    def group_of(turn):
+        return jnp.where(x == 0, jnp.where(turn >= skipped, turn + 1, turn), turn)
+
+    def x_step(step):
+        group, chunk = group_of(step // chunks), step % chunks
+        offset = (PAIR * (target(group) - z + depth) + 1 - 2 * x) % (PAIR * depth)
+        x_out[group, chunk] = partial(offset, chunk)
+        x_copy(group, chunk).start()
+
+    def z_copy(side, dest, chunk, stage, there):
+        return pltpu.make_async_remote_copy(
+            src_ref=z_out.at[stage, chunk],
+            dst_ref=z_in.at[side, dest, chunk],
+            send_sem=z_send.at[stage, chunk],
+            recv_sem=z_recv.at[side, dest, chunk],
+            device_id={"site": there},
+            device_id_type=MESH,
+        )
+
+    def arrived(side, dest, chunk):
+        z_copy(side, dest, chunk, 0, (site + PAIR) % (PAIR * depth)).wait_recv()
+        return z_in[side, dest, chunk]
+
+    def z_step(step):
+        stage, chunk = step // chunks, step % chunks
+        dest = target(stage)
+        up = dest > z
+        side = jnp.where(up, 0, 1)
+        offset = PAIR * ((dest - z + depth) % depth)
+        z_out[stage, chunk] = partial(offset, chunk)
+
+        @pl.when(jnp.logical_or(x == 0, stage != skipped))
+        def _():
+            x_copy(stage, chunk).wait_recv()
+            z_out[stage, chunk] = z_out[stage, chunk] + x_in[stage, chunk]
+
+        @pl.when(jnp.where(up, z, depth - 1 - z) > 0)
+        def _():
+            z_out[stage, chunk] = z_out[stage, chunk] + arrived(side, dest, chunk)
+
+        z_copy(side, dest, chunk, stage, jnp.where(up, site + PAIR, site - PAIR)).start()
+
+    def last_step(chunk):
+        spare = z_out.at[stages, 0]
+        spare[...] = partial(0, chunk)
+
+        @pl.when(x == 1)
+        def _():
+            x_copy(stages, chunk).wait_recv()
+            spare[...] = spare[...] + x_in[stages, chunk]
+
+        @pl.when(z > 0)
+        def _():
+            spare[...] = spare[...] + arrived(0, z, chunk)
+
+        @pl.when(z < depth - 1)
+        def _():
+            spare[...] = spare[...] + arrived(1, z, chunk)
+
+        rounded = spare[...].astype(jnp.bfloat16)
+        field_out[pl.ds(pl.multiple_of(chunk * ROWS, ROWS), ROWS), :] = rounded
+
+        def column(ref):
+            line = ref[pl.ds(chunk, 1), :]
+            return jnp.broadcast_to(line, (ROWS, ROWS)).T[:, :1]
+
+        log_yield = jnp.log(column(critical))
+        log_peak = column(median) + column(spread) * rounded.astype(jnp.float32)
+        log_ratio = log_yield - log_peak
+        margin = jnp.maximum(1.0 - jnp.exp(log_ratio), 0.0)
+        displacement = coeff_disp * jnp.exp(power_margin * jnp.log(margin) - power_ratio * log_ratio)
+        damage = jnp.log1p(displacement)
+        folded = damage[:, :ROWS]
+        for piece in range(1, own_reals // ROWS):
+            folded = folded + damage[:, piece * ROWS:(piece + 1) * ROWS]
+        totals[me, pl.ds(chunk, 1), :] = jnp.sum(folded.T, axis=0, keepdims=True)
+
+    @pl.loop(0, min(AHEAD, steps))
+    def _(step):
+        x_step(step)
+
+    @pl.loop(0, steps)
+    def _(step):
+        if AHEAD < steps:
+            @pl.when(step + AHEAD < steps)
+            def _():
+                x_step(step + AHEAD)
+
+        z_step(step)
+
+        @pl.when(step >= steps - chunks + LAG)
+        def _():
+            last_step(step - (steps - chunks + LAG))
+
+    @pl.loop(chunks - LAG, chunks)
+    def _(chunk):
+        last_step(chunk)
+
+    def t_copy(shift):
+        return pltpu.make_async_remote_copy(
+            src_ref=totals.at[me],
+            dst_ref=totals.at[me],
+            send_sem=t_send.at[shift],
+            recv_sem=t_recv.at[shift],
+            device_id={"real": (me + shift) % reals},
+            device_id_type=MESH,
+        )
+
+    for shift in range(1, reals):
+        t_copy(shift).start()
+
+    @pl.loop(0, steps)
+    def _(step):
+        x_copy(group_of(step // chunks), step % chunks).wait_send()
+        z_copy(0, 0, step % chunks, step // chunks, (site + PAIR) % (PAIR * depth)).wait_send()
+
+    for shift in range(1, reals):
+        t_copy(shift).wait()
+    total = totals[0]
+    for source in range(1, reals):
+        total = total + totals[source]
+    mean_out[...] = total / (own_reals * reals)
+
+
+def line_shards(epsilon, factor, block_rows, median_log, spread_log, critical_yield):
+    panels, per_column, tile = factor.shape[:3]
+    sites, own_reals = epsilon.shape
+    count, reals = lax.axis_size("site"), lax.axis_size("real")
+    depth = count // PAIR
+    chunks = sites // ROWS
+    relative = (block_rows - lax.axis_index("site") * panels) % (panels * count)
+    slots = jnp.arange((BAND // 2 + 1) * panels, dtype=jnp.int32)
+    hits = (relative[:, :, None] == slots).astype(jnp.int32)
+    numbers = jnp.arange(per_column, dtype=jnp.int32)[None, :, None]
+    table = jnp.concatenate([jnp.sum(hits * numbers, axis=1), jnp.sum(hits, axis=1)], axis=0)
+    piece = (ROWS, own_reals)
+    vmem = pl.BlockSpec(memory_space=pltpu.VMEM)
+    anywhere = pl.BlockSpec(memory_space=pl.ANY)
+    field, mean = pl.pallas_call(
+        functools.partial(field_kernel, depth, own_reals),
+        out_shape=(
+            jax.ShapeDtypeStruct((sites, own_reals), jnp.bfloat16),
+            jax.ShapeDtypeStruct((chunks, ROWS), jnp.float32),
+        ),
+        in_specs=[pl.BlockSpec(memory_space=pltpu.SMEM), anywhere, anywhere, vmem, vmem, vmem],
+        out_specs=(vmem, vmem),
+        scratch_shapes=[
+            pltpu.VMEM(epsilon.shape, epsilon.dtype),
+            pltpu.VMEM(factor.shape, factor.dtype),
+            pltpu.VMEM((depth, chunks) + piece, jnp.float32),
+            pltpu.VMEM((depth, chunks) + piece, jnp.float32),
+            pltpu.VMEM((depth, chunks) + piece, jnp.float32),
+            pltpu.VMEM((2, depth, chunks) + piece, jnp.float32),
+            pltpu.VMEM((reals, chunks, ROWS), jnp.float32),
+            pltpu.SemaphoreType.DMA((1 + panels,)),
+            pltpu.SemaphoreType.DMA((depth, chunks)),
+            pltpu.SemaphoreType.DMA((depth, chunks)),
+            pltpu.SemaphoreType.DMA((depth, chunks)),
+            pltpu.SemaphoreType.DMA((2, depth, chunks)),
+            pltpu.SemaphoreType.DMA((reals,)),
+            pltpu.SemaphoreType.DMA((reals,)),
+        ],
+        compiler_params=pltpu.CompilerParams(
+            collective_id=0, has_side_effects=True, vmem_limit_bytes=60 * 1024 * 1024
+        ),
+    )(
+        table,
+        epsilon,
+        factor,
+        median_log.reshape(chunks, ROWS),
+        spread_log.reshape(chunks, ROWS),
+        critical_yield.reshape(chunks, ROWS),
+    )
+    return field, mean.reshape(sites)
+
+
 def solution(mesh):
+    body = line_shards if mesh.shape["site"] == BAND // 2 + PAIR else shards
     return jax.shard_map(
-        shards,
+        body,
         mesh=mesh,
         in_specs=(
             P("site", "real"),

time: 467 us -> 163 us (0.35)
  the two profiles are of different devices: /device:TPU:10 before, /device:TPU:17 now
where the time goes in v1:
time: 163 us; the launch traced here: 162 us
  Pallas kernels  156 us (96%)
  local copies, waits for them, and re-layouts  3.63 us (2%)
    pallas_call x1, Pallas kernels, line_shards(): pl.pallas_call(functools.partial(field_kernel, depth, own_reals), out_sha...  156 us
    unnamed x2, local copies, waits for them, and re-layouts  3.53 us

profile of v1, /device:TPU:17, one launch (start us, length us, event | category | flops | bytes accessed | tf_op | source)
XLA Modules:
  0.0 161.9 jit_solution(9834146488379102836)
XLA Ops:
  0.6 0.7 and_select_fusion
  1.3 0.1 copy.8
  1.4 0.1 select_reduce_fusion
  1.5 0.6 pad_add_fusion.table
  2.1 156.2 %shard_map.77 = (bf16[1024,512]{1,0:T(8,128)(2,1)}, f32[8,128]{1,0:T(8,128)}) custom-call(s32[4,14]{1,0:T(4,128)} %pad_add_fusion.table, bf16[1024,512]{1,0:T(8,128)(2,1)} %eps_in.1, bf16[2,9,512,512]{3,2,1,0:T(8,128)(2,1)} %factor_in.1, f32[8,128]{1,0:T(8,128)} %bitcast.4, f32[8,128]{1,0:T(8,128)} %bitcast.5, f32[8,128]{1,0:T(8,128)} %bitcast.6), custom_call_target="tpu_custom_call" | custom-call | tf_op jit(solution)/shard_map/pallas_call | solution.py:274
  158.3 2.3 %copy.11 = bf16[1024,512]{1,0:T(8,128)(2,1)} copy(bf16[1024,512]{1,0:T(8,128)(2,1)} %get-tuple-element.10) | data formatting | bytes 2097152
  160.6 1.3 copy.12

commit v2 on v1

--- a/solution.py
+++ b/solution.py
@@ -9,7 +9,7 @@
 BAND = 12
 PAIR = 2
 ROWS = 128
-AHEAD = 24
+AHEAD = 4
 LAG = 1
 MESH = pl.DeviceIdType.MESH
 

time: 163 us -> 163 us (level)
  no operation moved by 1% of the time
where the time goes in v2:
time: 163 us; the launch traced here: 162 us
  Pallas kernels  156 us (96%)
  local copies, waits for them, and re-layouts  3.63 us (2%)
    pallas_call x1, Pallas kernels, line_shards(): pl.pallas_call(functools.partial(field_kernel, depth, own_reals), out_sha...  156 us
    unnamed x2, local copies, waits for them, and re-layouts  3.53 us

profile of v2, /device:TPU:17, one launch (start us, length us, event | category | flops | bytes accessed | tf_op | source)
XLA Modules:
  0.0 161.6 jit_solution(8693073408450493139)
XLA Ops:
  0.6 0.7 and_select_fusion
  1.3 0.1 copy.8
  1.4 0.1 select_reduce_fusion
  1.5 0.6 pad_add_fusion.table
  2.1 156.0 %shard_map.77 = (bf16[1024,512]{1,0:T(8,128)(2,1)}, f32[8,128]{1,0:T(8,128)}) custom-call(s32[4,14]{1,0:T(4,128)} %pad_add_fusion.table, bf16[1024,512]{1,0:T(8,128)(2,1)} %eps_in.1, bf16[2,9,512,512]{3,2,1,0:T(8,128)(2,1)} %factor_in.1, f32[8,128]{1,0:T(8,128)} %bitcast.4, f32[8,128]{1,0:T(8,128)} %bitcast.5, f32[8,128]{1,0:T(8,128)} %bitcast.6), custom_call_target="tpu_custom_call" | custom-call | tf_op jit(solution)/shard_map/pallas_call | solution.py:274
  158.1 2.3 %copy.11 = bf16[1024,512]{1,0:T(8,128)(2,1)} copy(bf16[1024,512]{1,0:T(8,128)(2,1)} %get-tuple-element.10) | data formatting | bytes 2097152
  160.3 1.3 copy.12

commit v3 on v2

--- a/solution.py
+++ b/solution.py
@@ -8,8 +8,11 @@
 
 BAND = 12
 PAIR = 2
-ROWS = 128
-AHEAD = 4
+LANES = 128
+ROWS = 64
+AHEAD = 6
+PARTS = 4
+HEAD = 2
 LAG = 1
 MESH = pl.DeviceIdType.MESH
 
@@ -62,8 +65,8 @@
 
 
 def field_kernel(
-    depth, own_reals, table, eps_in, factor_in, median, spread, critical, field_out, mean_out,
-    eps, factor, x_out, x_in, z_out, z_in, totals,
+    depth, own_reals, block_rows, eps_in, factor_in, median, spread, critical, field_out, mean_out,
+    eps, factor, head, x_out, x_in, z_out, z_in, totals, columns, folds, table,
     load_sem, x_send, x_recv, z_send, z_recv, t_send, t_recv,
 ):
     panels, per_column, tile = factor.shape[0], factor.shape[1], factor.shape[2]
@@ -76,10 +79,16 @@
     me = lax.axis_index("real")
     z, x = site // PAIR, site % PAIR
 
-    loads = [pltpu.make_async_copy(eps_in, eps, load_sem.at[0])]
+    first = [pltpu.make_async_copy(eps_in, eps, load_sem.at[0])]
+    rest = []
     for panel in range(panels):
-        loads.append(pltpu.make_async_copy(factor_in.at[panel], factor.at[panel], load_sem.at[1 + panel]))
-    for load in loads:
+        first.append(pltpu.make_async_copy(
+            factor_in.at[panel, :, :head.shape[2], :], head.at[panel], load_sem.at[1 + panel]
+        ))
+        rest.append(pltpu.make_async_copy(
+            factor_in.at[panel], factor.at[panel], load_sem.at[1 + panels + panel]
+        ))
+    for load in first + rest:
         load.start()
 
     barrier = pltpu.get_barrier_semaphore()
@@ -95,17 +104,40 @@
     def _():
         pl.semaphore_signal(barrier, inc=1, device_id={"site": site + PAIR}, device_id_type=MESH)
 
+    for panel in range(panels):
+        begins = [
+            (block_rows[panel, block] - site * panels + panels * PAIR * depth) % (panels * PAIR * depth)
+            for block in range(per_column)
+        ]
+
+        @pl.loop(0, table.shape[1])
+        def _(slot):
+            number, found = jnp.int32(0), jnp.int32(0)
+            for block in range(per_column):
+                hit = begins[block] == slot
+                number = jnp.where(hit, block, number)
+                found = jnp.where(hit, 1, found)
+            table[panel, slot] = number
+            table[panels + panel, slot] = found
+
+    for index, ref in enumerate((median, spread, critical)):
+        for line in range(panels * tile // LANES):
+            spot = slice(line * LANES, (line + 1) * LANES)
+            value = ref[line:line + 1, :]
+            value = jnp.log(value) if index == 2 else value
+            columns[index, spot, :] = jnp.broadcast_to(value, (LANES, LANES)).T
+
     pl.semaphore_wait(barrier, reals + jnp.where(z > 0, 1, 0) + jnp.where(z < depth - 1, 1, 0))
 
-    for load in loads:
+    for load in first:
         load.wait()
 
-    def partial(offset, chunk):
+    def partial(offset, chunk, source=factor):
         relative = panels * offset + chunk // per_tile
         row = pl.multiple_of((chunk % per_tile) * ROWS, ROWS)
         result = None
         for panel in range(panels):
-            block = factor[panel, table[panel, relative], pl.ds(row, ROWS), :]
+            block = source[panel, table[panel, relative], pl.ds(row, ROWS), :]
             product = jnp.dot(
                 block, eps[panel * tile:(panel + 1) * tile, :], preferred_element_type=jnp.float32
             ) * table[panels + panel, relative].astype(jnp.float32)
@@ -136,10 +168,10 @@
     def group_of(turn):
         return jnp.where(x == 0, jnp.where(turn >= skipped, turn + 1, turn), turn)
 
-    def x_step(step):
+    def x_step(step, source=factor):
         group, chunk = group_of(step // chunks), step % chunks
         offset = (PAIR * (target(group) - z + depth) + 1 - 2 * x) % (PAIR * depth)
-        x_out[group, chunk] = partial(offset, chunk)
+        x_out[group, chunk] = partial(offset, chunk, source)
         x_copy(group, chunk).start()
 
     def z_copy(side, dest, chunk, stage, there):
@@ -193,33 +225,39 @@
             spare[...] = spare[...] + arrived(1, z, chunk)
 
         rounded = spare[...].astype(jnp.bfloat16)
-        field_out[pl.ds(pl.multiple_of(chunk * ROWS, ROWS), ROWS), :] = rounded
-
-        def column(ref):
-            line = ref[pl.ds(chunk, 1), :]
-            return jnp.broadcast_to(line, (ROWS, ROWS)).T[:, :1]
-
-        log_yield = jnp.log(column(critical))
-        log_peak = column(median) + column(spread) * rounded.astype(jnp.float32)
-        log_ratio = log_yield - log_peak
-        margin = jnp.maximum(1.0 - jnp.exp(log_ratio), 0.0)
-        displacement = coeff_disp * jnp.exp(power_margin * jnp.log(margin) - power_ratio * log_ratio)
-        damage = jnp.log1p(displacement)
-        folded = damage[:, :ROWS]
-        for piece in range(1, own_reals // ROWS):
-            folded = folded + damage[:, piece * ROWS:(piece + 1) * ROWS]
-        totals[me, pl.ds(chunk, 1), :] = jnp.sum(folded.T, axis=0, keepdims=True)
-
-    @pl.loop(0, min(AHEAD, steps))
+        rows = pl.ds(pl.multiple_of(chunk * ROWS, ROWS), ROWS)
+        field_out[rows, :] = rounded
+        folded = None
+        for piece in range(own_reals // LANES):
+            residual = rounded[:, piece * LANES:(piece + 1) * LANES].astype(jnp.float32)
+            log_peak = columns[0, rows, :] + columns[1, rows, :] * residual
+            log_ratio = columns[2, rows, :] - log_peak
+            margin = jnp.maximum(1.0 - jnp.exp(log_ratio), 0.0)
+            displacement = coeff_disp * jnp.exp(power_margin * jnp.log(margin) - power_ratio * log_ratio)
+            damage = jnp.log1p(displacement)
+            folded = damage if folded is None else folded + damage
+        folds[rows, :] = folded
+
+        @pl.when((chunk + 1) % (LANES // ROWS) == 0)
+        def _():
+            line = chunk // (LANES // ROWS)
+            group = folds[pl.ds(pl.multiple_of(line * LANES, LANES), LANES), :]
+            totals[me, pl.ds(line, 1), :] = jnp.sum(group.T, axis=0, keepdims=True)
+
+    for step in range(HEAD):
+        x_step(step, head)
+    for load in rest:
+        load.wait()
+
+    @pl.loop(HEAD, AHEAD)
     def _(step):
         x_step(step)
 
     @pl.loop(0, steps)
     def _(step):
-        if AHEAD < steps:
-            @pl.when(step + AHEAD < steps)
-            def _():
-                x_step(step + AHEAD)
+        @pl.when(step + AHEAD < steps)
+        def _():
+            x_step(step + AHEAD)
 
         z_step(step)
 
@@ -257,17 +295,30 @@
     mean_out[...] = total / (own_reals * reals)
 
 
+def hand_out_kernel(field_in, mean_in, field_out, mean_out, field, mean, in_sem, out_sem):
+    part = field.shape[1]
+    reads = [pltpu.make_async_copy(mean_in, mean, in_sem.at[PARTS])]
+    writes = [pltpu.make_async_copy(mean, mean_out, out_sem.at[PARTS])]
+    for index in range(PARTS):
+        rows = pl.ds(index * part, part)
+        reads.append(pltpu.make_async_copy(field_in.at[rows, :], field.at[index], in_sem.at[index]))
+        writes.append(pltpu.make_async_copy(field.at[index], field_out.at[rows, :], out_sem.at[index]))
+    for read in reads:
+        read.start()
+    for read, write in zip(reads, writes):
+        read.wait()
+        write.start()
+    for write in writes:
+        write.wait()
+
+
 def line_shards(epsilon, factor, block_rows, median_log, spread_log, critical_yield):
     panels, per_column, tile = factor.shape[:3]
     sites, own_reals = epsilon.shape
     count, reals = lax.axis_size("site"), lax.axis_size("real")
     depth = count // PAIR
     chunks = sites // ROWS
-    relative = (block_rows - lax.axis_index("site") * panels) % (panels * count)
-    slots = jnp.arange((BAND // 2 + 1) * panels, dtype=jnp.int32)
-    hits = (relative[:, :, None] == slots).astype(jnp.int32)
-    numbers = jnp.arange(per_column, dtype=jnp.int32)[None, :, None]
-    table = jnp.concatenate([jnp.sum(hits * numbers, axis=1), jnp.sum(hits, axis=1)], axis=0)
+    lines = sites // LANES
     piece = (ROWS, own_reals)
     vmem = pl.BlockSpec(memory_space=pltpu.VMEM)
     anywhere = pl.BlockSpec(memory_space=pl.ANY)
@@ -275,19 +326,23 @@
         functools.partial(field_kernel, depth, own_reals),
         out_shape=(
             jax.ShapeDtypeStruct((sites, own_reals), jnp.bfloat16),
-            jax.ShapeDtypeStruct((chunks, ROWS), jnp.float32),
+            jax.ShapeDtypeStruct((lines, LANES), jnp.float32),
         ),
         in_specs=[pl.BlockSpec(memory_space=pltpu.SMEM), anywhere, anywhere, vmem, vmem, vmem],
         out_specs=(vmem, vmem),
         scratch_shapes=[
             pltpu.VMEM(epsilon.shape, epsilon.dtype),
             pltpu.VMEM(factor.shape, factor.dtype),
+            pltpu.VMEM((panels, per_column, HEAD * ROWS, tile), factor.dtype),
             pltpu.VMEM((depth, chunks) + piece, jnp.float32),
             pltpu.VMEM((depth, chunks) + piece, jnp.float32),
             pltpu.VMEM((depth, chunks) + piece, jnp.float32),
             pltpu.VMEM((2, depth, chunks) + piece, jnp.float32),
-            pltpu.VMEM((reals, chunks, ROWS), jnp.float32),
-            pltpu.SemaphoreType.DMA((1 + panels,)),
+            pltpu.VMEM((reals, lines, LANES), jnp.float32),
+            pltpu.VMEM((3, sites, LANES), jnp.float32),
+            pltpu.VMEM((sites, LANES), jnp.float32),
+            pltpu.SMEM((2 * panels, (BAND // 2 + 1) * panels), jnp.int32),
+            pltpu.SemaphoreType.DMA((1 + 2 * panels,)),
             pltpu.SemaphoreType.DMA((depth, chunks)),
             pltpu.SemaphoreType.DMA((depth, chunks)),
             pltpu.SemaphoreType.DMA((depth, chunks)),
@@ -299,13 +354,28 @@
             collective_id=0, has_side_effects=True, vmem_limit_bytes=60 * 1024 * 1024
         ),
     )(
-        table,
+        block_rows,
         epsilon,
         factor,
-        median_log.reshape(chunks, ROWS),
-        spread_log.reshape(chunks, ROWS),
-        critical_yield.reshape(chunks, ROWS),
+        median_log.reshape(lines, LANES),
+        spread_log.reshape(lines, LANES),
+        critical_yield.reshape(lines, LANES),
     )
+    field, mean = pl.pallas_call(
+        hand_out_kernel,
+        out_shape=(
+            jax.ShapeDtypeStruct(field.shape, field.dtype),
+            jax.ShapeDtypeStruct(mean.shape, mean.dtype),
+        ),
+        in_specs=[anywhere, anywhere],
+        out_specs=(anywhere, anywhere),
+        scratch_shapes=[
+            pltpu.VMEM((PARTS, sites // PARTS, own_reals), field.dtype),
+            pltpu.VMEM(mean.shape, mean.dtype),
+            pltpu.SemaphoreType.DMA((PARTS + 1,)),
+            pltpu.SemaphoreType.DMA((PARTS + 1,)),
+        ],
+    )(field, mean)
     return field, mean.reshape(sites)
 
 

time: 163 us -> 159 us (0.975); the launches traced: 162 us -> 159 us
  local copies, waits for them, and re-layouts: 3.63 us -> 0 us
  Pallas kernels: 156 us -> 159 us
    unnamed x2 -> x0, local copies, waits for them, and re-layouts: 3.53 us -> none
    pallas_call x0 -> x1, Pallas kernels: none -> 2 us  [line_shards(): pl.pallas_call(hand_out_kernel, out_shape=(jax.ShapeDtypeStruct(field.sha...]
where the time goes in v3:
time: 159 us
  Pallas kernels  159 us (100%)
    pallas_call x1, Pallas kernels, line_shards(): pl.pallas_call(functools.partial(field_kernel, depth, own_reals), out_sha...  157 us

profile of v3, /device:TPU:17, one launch (start us, length us, event | category | flops | bytes accessed | tf_op | source)
XLA Modules:
  0.0 159.2 jit_solution(17803391769290231801)
XLA Ops:
  0.6 156.6 %shard_map.77 = (bf16[1024,512]{1,0:T(8,128)(2,1)}, f32[8,128]{1,0:T(8,128)}) custom-call(s32[2,9]{1,0:T(2,128)} %block_rows.1, bf16[1024,512]{1,0:T(8,128)(2,1)} %eps_in.1, bf16[2,9,512,512]{3,2,1,0:T(8,128)(2,1)} %factor_in.1, f32[8,128]{1,0:T(8,128)} %bitcast.4, f32[8,128]{1,0:T(8,128)} %bitcast.5, f32[8,128]{1,0:T(8,128)} %bitcast.6), custom_call_target="tpu_custom_call" | custom-call | tf_op jit(solution)/shard_map/pallas_call | solution.py:325
  157.2 2.0 %shard_map.78 = (bf16[1024,512]{1,0:T(8,128)(2,1)}, f32[8,128]{1,0:T(8,128)}) custom-call(bf16[1024,512]{1,0:T(8,128)(2,1)} %get-tuple-element.6.field_in, f32[8,128]{1,0:T(8,128)} %get-tuple-element.7.mean_in), custom_call_target="tpu_custom_call" | custom-call | tf_op jit(solution)/shard_map/pallas_call | solution.py:364

commit v4 on v3

--- a/solution.py
+++ b/solution.py
@@ -120,13 +120,6 @@
             table[panel, slot] = number
             table[panels + panel, slot] = found
 
-    for index, ref in enumerate((median, spread, critical)):
-        for line in range(panels * tile // LANES):
-            spot = slice(line * LANES, (line + 1) * LANES)
-            value = ref[line:line + 1, :]
-            value = jnp.log(value) if index == 2 else value
-            columns[index, spot, :] = jnp.broadcast_to(value, (LANES, LANES)).T
-
     pl.semaphore_wait(barrier, reals + jnp.where(z > 0, 1, 0) + jnp.where(z < depth - 1, 1, 0))
 
     for load in first:
@@ -252,6 +245,13 @@
     @pl.loop(HEAD, AHEAD)
     def _(step):
         x_step(step)
+
+    for index, ref in enumerate((median, spread, critical)):
+        for line in range(panels * tile // LANES):
+            spot = slice(line * LANES, (line + 1) * LANES)
+            value = ref[line:line + 1, :]
+            value = jnp.log(value) if index == 2 else value
+            columns[index, spot, :] = jnp.broadcast_to(value, (LANES, LANES)).T
 
     @pl.loop(0, steps)
     def _(step):

time: 159 us -> 159 us (level)
  no operation moved by 1% of the time
where the time goes in v4:
time: 159 us
  Pallas kernels  159 us (100%)
    pallas_call x1, Pallas kernels, line_shards(): pl.pallas_call(functools.partial(field_kernel, depth, own_reals), out_sha...  157 us

profile of v4, /device:TPU:17, one launch (start us, length us, event | category | flops | bytes accessed | tf_op | source)
XLA Modules:
  0.0 159.2 jit_solution(1856237551931136986)
XLA Ops:
  0.6 156.6 %shard_map.77 = (bf16[1024,512]{1,0:T(8,128)(2,1)}, f32[8,128]{1,0:T(8,128)}) custom-call(s32[2,9]{1,0:T(2,128)} %block_rows.1, bf16[1024,512]{1,0:T(8,128)(2,1)} %eps_in.1, bf16[2,9,512,512]{3,2,1,0:T(8,128)(2,1)} %factor_in.1, f32[8,128]{1,0:T(8,128)} %bitcast.4, f32[8,128]{1,0:T(8,128)} %bitcast.5, f32[8,128]{1,0:T(8,128)} %bitcast.6), custom_call_target="tpu_custom_call" | custom-call | tf_op jit(solution)/shard_map/pallas_call | solution.py:325
  157.2 2.0 %shard_map.78 = (bf16[1024,512]{1,0:T(8,128)(2,1)}, f32[8,128]{1,0:T(8,128)}) custom-call(bf16[1024,512]{1,0:T(8,128)(2,1)} %get-tuple-element.6.field_in, f32[8,128]{1,0:T(8,128)} %get-tuple-element.7.mean_in), custom_call_target="tpu_custom_call" | custom-call | tf_op jit(solution)/shard_map/pallas_call | solution.py:364

commit v5 on v4

--- a/solution.py
+++ b/solution.py
@@ -66,8 +66,8 @@
 
 def field_kernel(
     depth, own_reals, block_rows, eps_in, factor_in, median, spread, critical, field_out, mean_out,
-    eps, factor, head, x_out, x_in, z_out, z_in, totals, columns, folds, table,
-    load_sem, x_send, x_recv, z_send, z_recv, t_send, t_recv,
+    eps, factor, head, x_out, x_in, z_out, z_in, totals, columns, folds, table, field,
+    load_sem, x_send, x_recv, z_send, z_recv, t_send, t_recv, f_send,
 ):
     panels, per_column, tile = factor.shape[0], factor.shape[1], factor.shape[2]
     chunks = panels * tile // ROWS
@@ -200,6 +200,10 @@
 
         z_copy(side, dest, chunk, stage, jnp.where(up, site + PAIR, site - PAIR)).start()
 
+    def field_copy(chunk):
+        rows = pl.ds(pl.multiple_of(chunk * ROWS, ROWS), ROWS)
+        return pltpu.make_async_copy(field.at[chunk], field_out.at[rows, :], f_send.at[chunk])
+
     def last_step(chunk):
         spare = z_out.at[stages, 0]
         spare[...] = partial(0, chunk)
@@ -219,7 +223,8 @@
 
         rounded = spare[...].astype(jnp.bfloat16)
         rows = pl.ds(pl.multiple_of(chunk * ROWS, ROWS), ROWS)
-        field_out[rows, :] = rounded
+        field[chunk] = rounded
+        field_copy(chunk).start()
         folded = None
         for piece in range(own_reals // LANES):
             residual = rounded[:, piece * LANES:(piece + 1) * LANES].astype(jnp.float32)
@@ -246,13 +251,6 @@
     def _(step):
         x_step(step)
 
-    for index, ref in enumerate((median, spread, critical)):
-        for line in range(panels * tile // LANES):
-            spot = slice(line * LANES, (line + 1) * LANES)
-            value = ref[line:line + 1, :]
-            value = jnp.log(value) if index == 2 else value
-            columns[index, spot, :] = jnp.broadcast_to(value, (LANES, LANES)).T
-
     @pl.loop(0, steps)
     def _(step):
         @pl.when(step + AHEAD < steps)
@@ -260,6 +258,14 @@
             x_step(step + AHEAD)
 
         z_step(step)
+
+        @pl.when(step < panels * tile // LANES)
+        def _():
+            spot = pl.ds(pl.multiple_of(step * LANES, LANES), LANES)
+            for index, ref in enumerate((median, spread, critical)):
+                value = ref[pl.ds(step, 1), :]
+                value = jnp.log(value) if index == 2 else value
+                columns[index, spot, :] = jnp.broadcast_to(value, (LANES, LANES)).T
 
         @pl.when(step >= steps - chunks + LAG)
         def _():
@@ -286,6 +292,10 @@
     def _(step):
         x_copy(group_of(step // chunks), step % chunks).wait_send()
         z_copy(0, 0, step % chunks, step // chunks, (site + PAIR) % (PAIR * depth)).wait_send()
+
+    @pl.loop(0, chunks)
+    def _(chunk):
+        field_copy(chunk).wait()
 
     for shift in range(1, reals):
         t_copy(shift).wait()
@@ -329,7 +339,7 @@
             jax.ShapeDtypeStruct((lines, LANES), jnp.float32),
         ),
         in_specs=[pl.BlockSpec(memory_space=pltpu.SMEM), anywhere, anywhere, vmem, vmem, vmem],
-        out_specs=(vmem, vmem),
+        out_specs=(anywhere, vmem),
         scratch_shapes=[
             pltpu.VMEM(epsilon.shape, epsilon.dtype),
             pltpu.VMEM(factor.shape, factor.dtype),
@@ -342,6 +352,7 @@
             pltpu.VMEM((3, sites, LANES), jnp.float32),
             pltpu.VMEM((sites, LANES), jnp.float32),
             pltpu.SMEM((2 * panels, (BAND // 2 + 1) * panels), jnp.int32),
+            pltpu.VMEM((chunks, ROWS, own_reals), jnp.bfloat16),
             pltpu.SemaphoreType.DMA((1 + 2 * panels,)),
             pltpu.SemaphoreType.DMA((depth, chunks)),
             pltpu.SemaphoreType.DMA((depth, chunks)),
@@ -349,6 +360,7 @@
             pltpu.SemaphoreType.DMA((2, depth, chunks)),
             pltpu.SemaphoreType.DMA((reals,)),
             pltpu.SemaphoreType.DMA((reals,)),
+            pltpu.SemaphoreType.DMA((chunks,)),
         ],
         compiler_params=pltpu.CompilerParams(
             collective_id=0, has_side_effects=True, vmem_limit_bytes=60 * 1024 * 1024

time: 159 us -> 159 us (level)
  no operation moved by 1% of the time
where the time goes in v5:
time: 159 us
  Pallas kernels  158 us (99%)
    pallas_call x1, Pallas kernels, line_shards(): pl.pallas_call(functools.partial(field_kernel, depth, own_reals), out_sha...  156 us

profile of v5, /device:TPU:17, one launch (start us, length us, event | category | flops | bytes accessed | tf_op | source)
XLA Modules:
  0.0 159.0 jit_solution(4838917016042175453)
XLA Ops:
  0.6 156.4 %shard_map.77 = (bf16[1024,512]{1,0:T(8,128)(2,1)}, f32[8,128]{1,0:T(8,128)}) custom-call(s32[2,9]{1,0:T(2,128)} %block_rows.1, bf16[1024,512]{1,0:T(8,128)(2,1)} %eps_in.1, bf16[2,9,512,512]{3,2,1,0:T(8,128)(2,1)} %factor_in.1, f32[8,128]{1,0:T(8,128)} %bitcast.4, f32[8,128]{1,0:T(8,128)} %bitcast.5, f32[8,128]{1,0:T(8,128)} %bitcast.6), custom_call_target="tpu_custom_call" | custom-call | tf_op jit(solution)/shard_map/pallas_call | solution.py:335
  157.0 2.0 %shard_map.78 = (bf16[1024,512]{1,0:T(8,128)(2,1)}, f32[8,128]{1,0:T(8,128)}) custom-call(bf16[1024,512]{1,0:T(8,128)(2,1)} %get-tuple-element.6.field_in, f32[8,128]{1,0:T(8,128)} %get-tuple-element.7.mean_in), custom_call_target="tpu_custom_call" | custom-call | tf_op jit(solution)/shard_map/pallas_call | solution.py:376
